TPU v7x, 256 devices: a whole 4x4x8 slice. The times are simulated.
256 devices in a mesh: section: 4 (over x_hi, core), tp: 2 (over x_lo), doc: 32 (over z, y).
Axes of the slice: x: 4 (x_hi: 2, x_lo: 2; x = x_hi * 2 + x_lo), y: 4, z: 8, core: 2. Of those that a mesh axis runs over, the one named last changes fastest.
Arguments:
- token_ids: int32 [64, 2, 32], P('doc'), may hold values from 0 to 16383
- seg_lengths: int32 [64, 2], P('doc'), may hold values from 1 to 32
- emb_table: bfloat16 [16384, 4096], P('section', 'tp'), may hold values from -6 to 6
- mem_init: bfloat16 [16, 4096], P(None, 'tp'), may hold values from -6 to 6
- norm_gain: float32 [4, 4096], P('section'), may hold values from 0.1 to 1.9
- w_query: bfloat16 [4, 4096, 2048], P('section', 'doc', 'tp'), may hold values from -0.09375 to 0.09375
- w_key: bfloat16 [4, 4096, 2048], P('section', 'doc', 'tp'), may hold values from -0.09375 to 0.09375
- w_value: bfloat16 [4, 4096, 2048], P('section', 'doc', 'tp'), may hold values from -0.09375 to 0.09375
- w_out: bfloat16 [4, 2048, 4096], P('section', None, 'tp'), may hold values from -0.125 to 0.125
- layer_mix: float32 [4], P('section'), may hold values from 0.5 to 4.5
Outputs:
- pooled: float32 [64, 4096], P(None, 'tp')
All inputs are finite; a program needn't handle non-finite values.
Results may differ from a plain program's by a relative error of at most 0.013.
Values may be sent and summed in bfloat16 or wider, within the bound.
A program may use at most 192 MiB of HBM per device.

v0:
```python
import math
import jax
import jax.numpy as jnp
from jax import lax
from jax.sharding import PartitionSpec as P

HD = 128
M = 16
L = 32
SEGS = 2
EPSILON = 1e-05
NEGATIVE = -1e30


def side_by_side(arrays, axis, dim, along):
    widths = [a.shape[along] for a in arrays]
    both = jnp.concatenate(arrays, axis=along)
    out = lax.all_gather(both, axis, axis=dim, tiled=True)
    return tuple(jnp.split(out, [sum(widths[:k]) for k in range(1, len(widths))], axis=along))


def from_behind(block, axis, distance):
    devices = range(lax.axis_size(axis))
    route = [((i - distance) % len(devices), i) for i in devices]
    return lax.ppermute(block, axis, route)


def laid_out(parts, dim):
    lengths = list(parts.shape[1:])
    lengths[dim] *= parts.shape[0]
    return jnp.moveaxis(parts, 0, dim).reshape(lengths)


def copy_for_each(shard, axis):
    copies = jnp.broadcast_to(shard, (lax.axis_size(axis), *shard.shape))
    return lax.all_to_all(copies, axis, split_axis=0, concat_axis=0, tiled=True)


def collect(shard, axis, dim):
    return laid_out(copy_for_each(shard, axis), dim)


def visible_rows(row_count, length):
    position = jnp.arange(row_count)
    key_ok = (position < M) | (position - M < length)
    ordered = (
        (position[None, :] < M) | (position[:, None] < M) | (position[None, :] <= position[:, None])
    )
    return key_ok[None, :] & ordered


def attend(features, length, query_proj, key_proj, value_proj, norm_row):
    row_count = features.shape[0]
    local_heads = query_proj.shape[1] // HD
    floats = features.astype(jnp.float32)
    mean_square = jnp.mean(floats * floats, -1, keepdims=True)
    normed = (floats * lax.rsqrt(mean_square + EPSILON) * norm_row).astype(jnp.bfloat16)
    head_shape = (row_count, local_heads, HD)
    queries = (
        jnp.dot(normed, query_proj, preferred_element_type=jnp.float32)
        .astype(jnp.bfloat16)
        .reshape(head_shape)
    )
    keys = (
        jnp.dot(normed, key_proj, preferred_element_type=jnp.float32)
        .astype(jnp.bfloat16)
        .reshape(head_shape)
    )
    values = (
        jnp.dot(normed, value_proj, preferred_element_type=jnp.float32)
        .astype(jnp.bfloat16)
        .reshape(head_shape)
    )
    scores = jnp.einsum("qhe,khe->hqk", queries, keys, preferred_element_type=jnp.float32) * (
        1.0 / math.sqrt(HD)
    )
    allowed = visible_rows(row_count, length)[None]
    scores = jnp.where(allowed, scores, NEGATIVE)
    weights = jnp.where(allowed, jnp.exp(scores), 0.0)
    probs = (weights / jnp.sum(weights, -1, keepdims=True)).astype(jnp.bfloat16)
    mixed = jnp.einsum("hqk,khe->qhe", probs, values, preferred_element_type=jnp.float32).astype(
        jnp.bfloat16
    )
    return mixed.reshape(row_count, local_heads * HD)


def body(
    token_ids,
    seg_lengths,
    emb_table,
    mem_init,
    norm_gain,
    w_query,
    w_key,
    w_value,
    w_out,
    layer_mix,
):
    phases = lax.axis_size("section")
    phase_index = lax.axis_index("section")
    doc_local = token_ids.shape[0]
    vocab_rows = emb_table.shape[0]
    width_local = emb_table.shape[1]
    flat_ids = token_ids.reshape(-1)
    local_ids = flat_ids - phase_index * vocab_rows
    owned = (local_ids >= 0) & (local_ids < vocab_rows)
    picked_rows = jnp.take(emb_table, jnp.clip(local_ids, 0, vocab_rows - 1), axis=0)
    partial_rows = jnp.where(owned[:, None], picked_rows.astype(jnp.float32), 0.0)
    embedded = lax.psum(partial_rows.astype(jnp.bfloat16), "section")
    embedded = embedded.reshape(doc_local * SEGS, L, width_local)
    query_proj, key_proj, value_proj = side_by_side((w_query[0], w_key[0], w_value[0]), "doc", 0, 1)
    out_proj = w_out[0]
    norm_row = norm_gain[0]
    mixing = layer_mix[0]
    row_count = M + L
    head_cols = query_proj.shape[1]
    total_turns = (SEGS - 1) * phases + doc_local + phases - 1

    def turn(turn_index, carried):
        incoming, returned, pooled = carried
        offset = turn_index - phase_index
        segment = offset // phases
        document = offset % phases
        active = (offset >= 0) & (document < doc_local) & (segment < SEGS)
        segment = jnp.clip(segment, 0, SEGS - 1)
        document = jnp.clip(document, 0, doc_local - 1)
        tokens = lax.dynamic_index_in_dim(embedded, document * SEGS + segment, 0, keepdims=False)
        earlier = incoming[:M]
        memory = jnp.where(segment == 0, mem_init, earlier)
        hidden = jnp.where(phase_index == 0, jnp.concatenate([memory, tokens], 0), incoming)
        length = seg_lengths[document, segment]
        features = lax.all_gather(hidden, "tp", axis=1, tiled=True)
        heads_out = lax.cond(
            active,
            lambda: attend(features, length, query_proj, key_proj, value_proj, norm_row),
            lambda: jnp.zeros((row_count, head_cols), jnp.bfloat16),
        )
        every_head = lax.all_gather(heads_out, "tp", axis=1, tiled=True)
        update = lax.cond(
            active,
            lambda: jnp.dot(every_head, out_proj, preferred_element_type=jnp.float32),
            lambda: jnp.zeros((row_count, width_local), jnp.float32),
        )
        result = (hidden.astype(jnp.float32) + update).astype(jnp.bfloat16)
        token_ok = jnp.arange(L) < length
        summed = jnp.sum(
            jnp.where(token_ok[:, None], result[M:].astype(jnp.float32), 0.0), 0
        ) / length.astype(jnp.float32)
        scale_now = jnp.where(active & (segment == SEGS - 1), mixing, 0.0)
        picked = (jnp.arange(doc_local) == document).astype(jnp.float32)
        pooled = pooled + picked[:, None] * (scale_now * summed)[None, :]
        incoming = from_behind(result, "section", 1)
        return (incoming, returned, pooled)

    start_state = (
        jnp.zeros((row_count, width_local), jnp.bfloat16),
        jnp.zeros((M, width_local), jnp.bfloat16),
        jnp.zeros((doc_local, width_local), jnp.float32),
    )
    final_state = lax.fori_loop(0, total_turns, turn, start_state)
    pooled = final_state[2]
    layer_total = lax.psum(pooled, "section")
    return collect(layer_total, "doc", 0)


def solution(mesh):
    return jax.shard_map(
        body,
        mesh=mesh,
        in_specs=(
            P("doc", None, None),
            P("doc", None),
            P("section", "tp"),
            P(None, "tp"),
            P("section", None),
            P("section", "doc", "tp"),
            P("section", "doc", "tp"),
            P("section", "doc", "tp"),
            P("section", None, "tp"),
            P("section"),
        ),
        out_specs=P(None, "tp"),
        check_vma=False,
    )
```

profile of v0, /device:TPU:6, one launch (start us, length us, event | category | flops | bytes accessed | tf_op | source)
XLA Modules:
  0.0 544.1 jit_solution(7246789136166503386)
XLA Ops:
  11.2 9.4 %gather_fusion = bf16[128,2048]{1,0:T(8,128)(2,1)S(1)} fusion(bf16[4096,2048]{1,0:T(8,128)(2,1)} %param.18, s32[1024]{0:T(1024)S(1)} %pad_clamp_fusion), kind=kCustom, calls=%fused_computation | custom fusion | bytes 1049088 | tf_op jit(solution)/shard_map/jit(_take)/gather | solution.py:107
  21.8 175.4 %all-gather.2.cloned.1.call-done = bf16[4096,3072]{1,0:T(8,128)(2,1)} async-done(((bf16[128,3072]{1,0:T(8,128)(2,1)}), bf16[4096,3072]{1,0:T(8,128)(2,1)}) %all-gather.2.cloned.1.call-update) | async-done | bytes 25165840 | tf_op jit(solution)/shard_map/all_gather | solution.py:18
  197.2 16.9 %fusion.25 = (bf16[4096,1024]{1,0:T(8,128)(2,1)}, bf16[4096,1024]{1,0:T(8,128)(2,1)}, bf16[4096,1024]{1,0:T(8,128)(2,1)}) fusion(bf16[4096,3072]{1,0:T(8,128)(2,1)} %all-gather.2.cloned.1.call-done), kind=kLoop, calls=%fused_computation.52 | loop fusion | bytes 50331648 | tf_op jit(solution)/shard_map/split | solution.py:19
  214.2 284.0 %while.18 = (s32[]{:T(128)}, bf16[48,2048]{1,0:T(8,128)(2,1)S(1)}, f32[2,2048]{1,0:T(2,128)S(1)}, pred[]{:T(512)}, s32[]{:T(128)}, /*index=5*/bf16[16,2048]{1,0:...) while((s32[]{:T(128)}, bf16[48,2048]{1,0:T(8,128)(2,1)S(1)}, ...), condition=%wide.region_9.10_spmd.clone, body=%wide.region_1.9_spmd.clone.sunk | while | flops 1624327808 | bytes 90839752 | solution.py:160
  215.2 6.6 %all_gather.28 = bf16[48,4096]{1,0:T(8,128)(2,1)S(1)} all-gather(bf16[48,2048]{1,0:T(8,128)(2,1)S(1)} %maximum_select_fusion.2), channel_id=1, replica_groups=mesh['section'=4,'tp'=2,'doc'=32] {'tp'}, dimensions={1}, use_global_device_ids=true | all-gather | bytes 589824 | tf_op jit(solution)/shard_map/while/body/eval_jaxpr/all_gather | solution.py:132
  222.4 5.3 all_gather.29
  235.5 6.3 %all_gather.28 = bf16[48,4096]{1,0:T(8,128)(2,1)S(1)} all-gather(bf16[48,2048]{1,0:T(8,128)(2,1)S(1)} %maximum_select_fusion.2), channel_id=1, replica_groups=mesh['section'=4,'tp'=2,'doc'=32] {'tp'}, dimensions={1}, use_global_device_ids=true | all-gather | bytes 589824 | tf_op jit(solution)/shard_map/while/body/eval_jaxpr/all_gather | solution.py:132
  242.5 6.3 %all_gather.29 = bf16[48,2048]{1,0:T(8,128)(2,1)S(1)} all-gather(bf16[48,1024]{1,0:T(8,128)(2,1)S(1)} %get-tuple-element.593), channel_id=1, replica_groups=mesh['section'=4,'tp'=2,'doc'=32] {'tp'}, dimensions={1}, use_global_device_ids=true | all-gather | bytes 294912 | tf_op jit(solution)/shard_map/while/body/eval_jaxpr/all_gather | solution.py:138
  248.8 10.6 %collective-permute-start = (bf16[48,2048]{1,0:T(8,128)(2,1)S(1)}, bf16[48,2048]{1,0:T(8,128)(2,1)S(1)}, u32[]{:S(2)}, u32[]{:S(2)}) collective-permute-start(bf16[48,2048]{1,0:T(8,128)(2,1)S(1)} %add_convert_fusion.2), channel_id=1, source_target_pairs={{192,0},{0,64},{64,128},{128,192},{193,1},{1,65},{65,129},{129,193... | collective-permute-start | bytes 589832 | tf_op jit(solution)/shard_map/while/body/eval_jaxpr/ppermute | solution.py:25
  261.6 15.0 %collective-permute-done = bf16[48,2048]{1,0:T(8,128)(2,1)S(1)} collective-permute-done((bf16[48,2048]{1,0:T(8,128)(2,1)S(1)}, bf16[48,2048]{1,0:T(8,128)(2,1)S(1)}, u32[]{:S(2)}, u32[]{:S(2)}) %collective-permute-start) | collective-permute-done | bytes 196640 | tf_op jit(solution)/shard_map/while/body/eval_jaxpr/ppermute | solution.py:25
  277.6 7.2 %all_gather.28 = bf16[48,4096]{1,0:T(8,128)(2,1)S(1)} all-gather(bf16[48,2048]{1,0:T(8,128)(2,1)S(1)} %maximum_select_fusion.2), channel_id=1, replica_groups=mesh['section'=4,'tp'=2,'doc'=32] {'tp'}, dimensions={1}, use_global_device_ids=true | all-gather | bytes 589824 | tf_op jit(solution)/shard_map/while/body/eval_jaxpr/all_gather | solution.py:132
  285.4 10.4 %conditional.6 = (bf16[48,1024]{1,0:T(8,128)(2,1)S(1)}) conditional(s32[]{:T(128)} %convert_element_type.148, () %tuple.64, (bf16[48,4096]{1,0:T(8,128)(2,1)S(1)}, f32[1,4096]{1,0:T(1,128)S(1)}, bf16[4096,1024]{1,0:T(8,128)(2,1)}, s32[]{:T(128)}, bf16[4096,1024]{1,0:T(8,128)(2,1)}, /*index=5*/bf16[4096,1024]{1,0:T(8,128)(2,1)}) %tuple.65), branch_computations={%region_2.2_spmd, %region_3.5_spmd} | conditional | flops 1220644480 | bytes 78157736 | solution.py:133
  285.7 5.2 fusion.5
  295.9 5.3 all_gather.29
  301.2 4.9 conditional.7
  301.2 4.9 fusion.26
  308.4 4.4 collective-permute-done
  313.9 6.3 %all_gather.28 = bf16[48,4096]{1,0:T(8,128)(2,1)S(1)} all-gather(bf16[48,2048]{1,0:T(8,128)(2,1)S(1)} %maximum_select_fusion.2), channel_id=1, replica_groups=mesh['section'=4,'tp'=2,'doc'=32] {'tp'}, dimensions={1}, use_global_device_ids=true | all-gather | bytes 589824 | tf_op jit(solution)/shard_map/while/body/eval_jaxpr/all_gather | solution.py:132
  320.8 10.4 %conditional.6 = (bf16[48,1024]{1,0:T(8,128)(2,1)S(1)}) conditional(s32[]{:T(128)} %convert_element_type.148, () %tuple.64, (bf16[48,4096]{1,0:T(8,128)(2,1)S(1)}, f32[1,4096]{1,0:T(1,128)S(1)}, bf16[4096,1024]{1,0:T(8,128)(2,1)}, s32[]{:T(128)}, bf16[4096,1024]{1,0:T(8,128)(2,1)}, /*index=5*/bf16[4096,1024]{1,0:T(8,128)(2,1)}) %tuple.65), branch_computations={%region_2.2_spmd, %region_3.5_spmd} | conditional | flops 1220644480 | bytes 78157736 | solution.py:133
  321.0 5.2 fusion.5
  331.3 6.3 %all_gather.29 = bf16[48,2048]{1,0:T(8,128)(2,1)S(1)} all-gather(bf16[48,1024]{1,0:T(8,128)(2,1)S(1)} %get-tuple-element.593), channel_id=1, replica_groups=mesh['section'=4,'tp'=2,'doc'=32] {'tp'}, dimensions={1}, use_global_device_ids=true | all-gather | bytes 294912 | tf_op jit(solution)/shard_map/while/body/eval_jaxpr/all_gather | solution.py:138
  337.6 4.9 conditional.7
  337.6 4.9 fusion.26
  344.8 5.1 collective-permute-done
  351.0 6.3 %all_gather.28 = bf16[48,4096]{1,0:T(8,128)(2,1)S(1)} all-gather(bf16[48,2048]{1,0:T(8,128)(2,1)S(1)} %maximum_select_fusion.2), channel_id=1, replica_groups=mesh['section'=4,'tp'=2,'doc'=32] {'tp'}, dimensions={1}, use_global_device_ids=true | all-gather | bytes 589824 | tf_op jit(solution)/shard_map/while/body/eval_jaxpr/all_gather | solution.py:132
  357.9 5.3 all_gather.29
  363.3 7.2 %collective-permute-start = (bf16[48,2048]{1,0:T(8,128)(2,1)S(1)}, bf16[48,2048]{1,0:T(8,128)(2,1)S(1)}, u32[]{:S(2)}, u32[]{:S(2)}) collective-permute-start(bf16[48,2048]{1,0:T(8,128)(2,1)S(1)} %add_convert_fusion.2), channel_id=1, source_target_pairs={{192,0},{0,64},{64,128},{128,192},{193,1},{1,65},{65,129},{129,193... | collective-permute-start | bytes 589832 | tf_op jit(solution)/shard_map/while/body/eval_jaxpr/ppermute | solution.py:25
  373.8 7.8 %all_gather.28 = bf16[48,4096]{1,0:T(8,128)(2,1)S(1)} all-gather(bf16[48,2048]{1,0:T(8,128)(2,1)S(1)} %maximum_select_fusion.2), channel_id=1, replica_groups=mesh['section'=4,'tp'=2,'doc'=32] {'tp'}, dimensions={1}, use_global_device_ids=true | all-gather | bytes 589824 | tf_op jit(solution)/shard_map/while/body/eval_jaxpr/all_gather | solution.py:132
  382.3 5.3 all_gather.29
  389.9 12.3 %collective-permute-done = bf16[48,2048]{1,0:T(8,128)(2,1)S(1)} collective-permute-done((bf16[48,2048]{1,0:T(8,128)(2,1)S(1)}, bf16[48,2048]{1,0:T(8,128)(2,1)S(1)}, u32[]{:S(2)}, u32[]{:S(2)}) %collective-permute-start) | collective-permute-done | bytes 196640 | tf_op jit(solution)/shard_map/while/body/eval_jaxpr/ppermute | solution.py:25
  403.2 7.1 %all_gather.28 = bf16[48,4096]{1,0:T(8,128)(2,1)S(1)} all-gather(bf16[48,2048]{1,0:T(8,128)(2,1)S(1)} %maximum_select_fusion.2), channel_id=1, replica_groups=mesh['section'=4,'tp'=2,'doc'=32] {'tp'}, dimensions={1}, use_global_device_ids=true | all-gather | bytes 589824 | tf_op jit(solution)/shard_map/while/body/eval_jaxpr/all_gather | solution.py:132
  410.9 10.4 %conditional.6 = (bf16[48,1024]{1,0:T(8,128)(2,1)S(1)}) conditional(s32[]{:T(128)} %convert_element_type.148, () %tuple.64, (bf16[48,4096]{1,0:T(8,128)(2,1)S(1)}, f32[1,4096]{1,0:T(1,128)S(1)}, bf16[4096,1024]{1,0:T(8,128)(2,1)}, s32[]{:T(128)}, bf16[4096,1024]{1,0:T(8,128)(2,1)}, /*index=5*/bf16[4096,1024]{1,0:T(8,128)(2,1)}) %tuple.65), branch_computations={%region_2.2_spmd, %region_3.5_spmd} | conditional | flops 1220644480 | bytes 78157736 | solution.py:133
  411.1 5.2 fusion.5
  421.3 5.3 all_gather.29
  426.6 4.9 conditional.7
  426.6 4.9 fusion.26
  439.3 6.3 %all_gather.28 = bf16[48,4096]{1,0:T(8,128)(2,1)S(1)} all-gather(bf16[48,2048]{1,0:T(8,128)(2,1)S(1)} %maximum_select_fusion.2), channel_id=1, replica_groups=mesh['section'=4,'tp'=2,'doc'=32] {'tp'}, dimensions={1}, use_global_device_ids=true | all-gather | bytes 589824 | tf_op jit(solution)/shard_map/while/body/eval_jaxpr/all_gather | solution.py:132
  446.2 10.4 %conditional.6 = (bf16[48,1024]{1,0:T(8,128)(2,1)S(1)}) conditional(s32[]{:T(128)} %convert_element_type.148, () %tuple.64, (bf16[48,4096]{1,0:T(8,128)(2,1)S(1)}, f32[1,4096]{1,0:T(1,128)S(1)}, bf16[4096,1024]{1,0:T(8,128)(2,1)}, s32[]{:T(128)}, bf16[4096,1024]{1,0:T(8,128)(2,1)}, /*index=5*/bf16[4096,1024]{1,0:T(8,128)(2,1)}) %tuple.65), branch_computations={%region_2.2_spmd, %region_3.5_spmd} | conditional | flops 1220644480 | bytes 78157736 | solution.py:133
  446.4 5.2 fusion.5
  456.7 6.3 %all_gather.29 = bf16[48,2048]{1,0:T(8,128)(2,1)S(1)} all-gather(bf16[48,1024]{1,0:T(8,128)(2,1)S(1)} %get-tuple-element.593), channel_id=1, replica_groups=mesh['section'=4,'tp'=2,'doc'=32] {'tp'}, dimensions={1}, use_global_device_ids=true | all-gather | bytes 294912 | tf_op jit(solution)/shard_map/while/body/eval_jaxpr/all_gather | solution.py:138
  463.0 4.9 conditional.7
  463.0 4.9 fusion.26
  470.3 5.1 collective-permute-done
  476.4 6.3 %all_gather.28 = bf16[48,4096]{1,0:T(8,128)(2,1)S(1)} all-gather(bf16[48,2048]{1,0:T(8,128)(2,1)S(1)} %maximum_select_fusion.2), channel_id=1, replica_groups=mesh['section'=4,'tp'=2,'doc'=32] {'tp'}, dimensions={1}, use_global_device_ids=true | all-gather | bytes 589824 | tf_op jit(solution)/shard_map/while/body/eval_jaxpr/all_gather | solution.py:132
  483.4 5.3 all_gather.29
  488.7 7.2 %collective-permute-start = (bf16[48,2048]{1,0:T(8,128)(2,1)S(1)}, bf16[48,2048]{1,0:T(8,128)(2,1)S(1)}, u32[]{:S(2)}, u32[]{:S(2)}) collective-permute-start(bf16[48,2048]{1,0:T(8,128)(2,1)S(1)} %add_convert_fusion.2), channel_id=1, source_target_pairs={{192,0},{0,64},{64,128},{128,192},{193,1},{1,65},{65,129},{129,193... | collective-permute-start | bytes 589832 | tf_op jit(solution)/shard_map/while/body/eval_jaxpr/ppermute | solution.py:25
  498.2 13.7 %psum.15 = f32[2,2048]{1,0:T(2,128)S(1)} all-reduce(f32[2,2048]{1,0:T(2,128)S(1)} %get-tuple-element.366), channel_id=1, replica_groups=mesh['section'=4,'tp'=2,'doc'=32] {'section'}, use_global_device_ids=true, to_apply=%region_10.11 | all-reduce | flops 4096 | bytes 32768 | tf_op jit(solution)/shard_map/psum | solution.py:162
  512.1 23.4 %all_to_all.5 = f32[32,2,2048]{2,1,0:T(2,128)S(1)} all-to-all(f32[32,2,2048]{2,1,0:T(2,128)S(1)} %broadcast_in_dim.106), channel_id=1, replica_groups=mesh['section'=4,'tp'=2,'doc'=32] {'doc'}, dimensions={0} | all-to-all | bytes 1048576 | tf_op jit(solution)/shard_map/all_to_all | solution.py:36
  (221 shorter events, 59.1 us)
Async XLA Ops:
  7.4 189.8 %all-gather.2.cloned.1.call-start = ((), (), s32[]{:S(2)}) async-start(), calls=%async_computation.2 | async-start | bytes 25952256 | tf_op jit(solution)/shard_map/all_gather | solution.py:18
  9.5 204.6 %all-reduce.2.cloned.1.call-start = ((), (), s32[]{:S(2)}) async-start(), calls=%async_computation.1 | async-start | bytes 1048576 | tf_op jit(solution)/shard_map/psum | solution.py:109
  21.7 192.4 %copy-start = (f32[1,4096]{1,0:T(1,128)S(1)}, f32[1,4096]{1,0:T(1,128)}, u32[]{:S(2)}) copy-start(f32[1,4096]{1,0:T(1,128)} %param.20) | copy-start | bytes 49156
  21.7 192.4 %copy-start.1 = (bf16[16,2048]{1,0:T(8,128)(2,1)S(1)}, bf16[16,2048]{1,0:T(8,128)(2,1)}, u32[]{:S(2)}) copy-start(bf16[16,2048]{1,0:T(8,128)(2,1)} %param.19) | copy-start | bytes 196612
  21.8 192.4 %copy-start.2 = (s32[2,2]{1,0:T(2,128)S(1)}, s32[2,2]{1,0:T(2,128)}, u32[]{:S(2)}) copy-start(s32[2,2]{1,0:T(2,128)} %param.17) | copy-start | bytes 52
  227.8 6.7 %collective-permute-start = (bf16[48,2048]{1,0:T(8,128)(2,1)S(1)}, bf16[48,2048]{1,0:T(8,128)(2,1)S(1)}, u32[]{:S(2)}, u32[]{:S(2)}) collective-permute-start(bf16[48,2048]{1,0:T(8,128)(2,1)S(1)} %add_convert_fusion.2), channel_id=1, source_target_pairs={{192,0},{0,64},{64,128},{128,192},{193,1},{1,65},{65,129},{129,193... | collective-permute-start | bytes 589832 | tf_op jit(solution)/shard_map/while/body/eval_jaxpr/ppermute | solution.py:25
  248.8 27.7 %collective-permute-start = (bf16[48,2048]{1,0:T(8,128)(2,1)S(1)}, bf16[48,2048]{1,0:T(8,128)(2,1)S(1)}, u32[]{:S(2)}, u32[]{:S(2)}) collective-permute-start(bf16[48,2048]{1,0:T(8,128)(2,1)S(1)} %add_convert_fusion.2), channel_id=1, source_target_pairs={{192,0},{0,64},{64,128},{128,192},{193,1},{1,65},{65,129},{129,193... | collective-permute-start | bytes 589832 | tf_op jit(solution)/shard_map/while/body/eval_jaxpr/ppermute | solution.py:25
  285.4 5.4 slice-start
  285.6 5.7 %slice-start.1 = ((s8[8388608]{0:T(1024)(128)(4,1)}), s8[4194304]{0:T(1024)(128)(4,1)S(1)}, s32[]{:S(2)}) async-start(s8[8388608]{0:T(1024)(128)(4,1)} %bitcast.43), calls=%async_computation.4 | async-start | bytes 8388608 | tf_op jit(solution)/shard_map/while/body/eval_jaxpr/cond
  285.6 8.3 %slice-start.2 = ((s8[8388608]{0:T(1024)(128)(4,1)}), s8[4194304]{0:T(1024)(128)(4,1)S(1)}, s32[]{:S(2)}) async-start(s8[8388608]{0:T(1024)(128)(4,1)} %bitcast.45), calls=%async_computation.5 | async-start | bytes 8388608 | tf_op jit(solution)/shard_map/while/body/eval_jaxpr/cond
  291.3 2.6 slice-start.3
  306.2 6.7 %collective-permute-start = (bf16[48,2048]{1,0:T(8,128)(2,1)S(1)}, bf16[48,2048]{1,0:T(8,128)(2,1)S(1)}, u32[]{:S(2)}, u32[]{:S(2)}) collective-permute-start(bf16[48,2048]{1,0:T(8,128)(2,1)S(1)} %add_convert_fusion.2), channel_id=1, source_target_pairs={{192,0},{0,64},{64,128},{128,192},{193,1},{1,65},{65,129},{129,193... | collective-permute-start | bytes 589832 | tf_op jit(solution)/shard_map/while/body/eval_jaxpr/ppermute | solution.py:25
  320.8 5.4 slice-start
  321.0 5.7 %slice-start.1 = ((s8[8388608]{0:T(1024)(128)(4,1)}), s8[4194304]{0:T(1024)(128)(4,1)S(1)}, s32[]{:S(2)}) async-start(s8[8388608]{0:T(1024)(128)(4,1)} %bitcast.43), calls=%async_computation.4 | async-start | bytes 8388608 | tf_op jit(solution)/shard_map/while/body/eval_jaxpr/cond
  321.0 8.3 %slice-start.2 = ((s8[8388608]{0:T(1024)(128)(4,1)}), s8[4194304]{0:T(1024)(128)(4,1)S(1)}, s32[]{:S(2)}) async-start(s8[8388608]{0:T(1024)(128)(4,1)} %bitcast.45), calls=%async_computation.5 | async-start | bytes 8388608 | tf_op jit(solution)/shard_map/while/body/eval_jaxpr/cond
  326.7 2.6 slice-start.3
  342.6 7.4 %collective-permute-start = (bf16[48,2048]{1,0:T(8,128)(2,1)S(1)}, bf16[48,2048]{1,0:T(8,128)(2,1)S(1)}, u32[]{:S(2)}, u32[]{:S(2)}) collective-permute-start(bf16[48,2048]{1,0:T(8,128)(2,1)S(1)} %add_convert_fusion.2), channel_id=1, source_target_pairs={{192,0},{0,64},{64,128},{128,192},{193,1},{1,65},{65,129},{129,193... | collective-permute-start | bytes 589832 | tf_op jit(solution)/shard_map/while/body/eval_jaxpr/ppermute | solution.py:25
  363.3 9.4 %collective-permute-start = (bf16[48,2048]{1,0:T(8,128)(2,1)S(1)}, bf16[48,2048]{1,0:T(8,128)(2,1)S(1)}, u32[]{:S(2)}, u32[]{:S(2)}) collective-permute-start(bf16[48,2048]{1,0:T(8,128)(2,1)S(1)} %add_convert_fusion.2), channel_id=1, source_target_pairs={{192,0},{0,64},{64,128},{128,192},{193,1},{1,65},{65,129},{129,193... | collective-permute-start | bytes 589832 | tf_op jit(solution)/shard_map/while/body/eval_jaxpr/ppermute | solution.py:25
  387.6 14.6 %collective-permute-start = (bf16[48,2048]{1,0:T(8,128)(2,1)S(1)}, bf16[48,2048]{1,0:T(8,128)(2,1)S(1)}, u32[]{:S(2)}, u32[]{:S(2)}) collective-permute-start(bf16[48,2048]{1,0:T(8,128)(2,1)S(1)} %add_convert_fusion.2), channel_id=1, source_target_pairs={{192,0},{0,64},{64,128},{128,192},{193,1},{1,65},{65,129},{129,193... | collective-permute-start | bytes 589832 | tf_op jit(solution)/shard_map/while/body/eval_jaxpr/ppermute | solution.py:25
  410.9 5.4 slice-start
  411.1 5.7 %slice-start.1 = ((s8[8388608]{0:T(1024)(128)(4,1)}), s8[4194304]{0:T(1024)(128)(4,1)S(1)}, s32[]{:S(2)}) async-start(s8[8388608]{0:T(1024)(128)(4,1)} %bitcast.43), calls=%async_computation.4 | async-start | bytes 8388608 | tf_op jit(solution)/shard_map/while/body/eval_jaxpr/cond
  411.1 8.3 %slice-start.2 = ((s8[8388608]{0:T(1024)(128)(4,1)}), s8[4194304]{0:T(1024)(128)(4,1)S(1)}, s32[]{:S(2)}) async-start(s8[8388608]{0:T(1024)(128)(4,1)} %bitcast.45), calls=%async_computation.5 | async-start | bytes 8388608 | tf_op jit(solution)/shard_map/while/body/eval_jaxpr/cond
  416.8 2.6 slice-start.3
  431.6 6.7 %collective-permute-start = (bf16[48,2048]{1,0:T(8,128)(2,1)S(1)}, bf16[48,2048]{1,0:T(8,128)(2,1)S(1)}, u32[]{:S(2)}, u32[]{:S(2)}) collective-permute-start(bf16[48,2048]{1,0:T(8,128)(2,1)S(1)} %add_convert_fusion.2), channel_id=1, source_target_pairs={{192,0},{0,64},{64,128},{128,192},{193,1},{1,65},{65,129},{129,193... | collective-permute-start | bytes 589832 | tf_op jit(solution)/shard_map/while/body/eval_jaxpr/ppermute | solution.py:25
  446.2 5.4 slice-start
  446.4 5.7 %slice-start.1 = ((s8[8388608]{0:T(1024)(128)(4,1)}), s8[4194304]{0:T(1024)(128)(4,1)S(1)}, s32[]{:S(2)}) async-start(s8[8388608]{0:T(1024)(128)(4,1)} %bitcast.43), calls=%async_computation.4 | async-start | bytes 8388608 | tf_op jit(solution)/shard_map/while/body/eval_jaxpr/cond
  446.4 8.3 %slice-start.2 = ((s8[8388608]{0:T(1024)(128)(4,1)}), s8[4194304]{0:T(1024)(128)(4,1)S(1)}, s32[]{:S(2)}) async-start(s8[8388608]{0:T(1024)(128)(4,1)} %bitcast.45), calls=%async_computation.5 | async-start | bytes 8388608 | tf_op jit(solution)/shard_map/while/body/eval_jaxpr/cond
  452.1 2.6 slice-start.3
  468.0 7.4 %collective-permute-start = (bf16[48,2048]{1,0:T(8,128)(2,1)S(1)}, bf16[48,2048]{1,0:T(8,128)(2,1)S(1)}, u32[]{:S(2)}, u32[]{:S(2)}) collective-permute-start(bf16[48,2048]{1,0:T(8,128)(2,1)S(1)} %add_convert_fusion.2), channel_id=1, source_target_pairs={{192,0},{0,64},{64,128},{128,192},{193,1},{1,65},{65,129},{129,193... | collective-permute-start | bytes 589832 | tf_op jit(solution)/shard_map/while/body/eval_jaxpr/ppermute | solution.py:25
  488.7 9.4 %collective-permute-start = (bf16[48,2048]{1,0:T(8,128)(2,1)S(1)}, bf16[48,2048]{1,0:T(8,128)(2,1)S(1)}, u32[]{:S(2)}, u32[]{:S(2)}) collective-permute-start(bf16[48,2048]{1,0:T(8,128)(2,1)S(1)} %add_convert_fusion.2), channel_id=1, source_target_pairs={{192,0},{0,64},{64,128},{128,192},{193,1},{1,65},{65,129},{129,193... | collective-permute-start | bytes 589832 | tf_op jit(solution)/shard_map/while/body/eval_jaxpr/ppermute | solution.py:25
Sparse Core Ops, SparseCore 0:
  10.7 186.3 all-gather.1
Sparse Core Ops, SparseCore 1:
  21.8 48.7 all-reduce.1
where the time goes:
time: 545 us; the launch traced here: 544 us
  waiting for transfers between devices  226 us (41%)
  blocking collectives  148 us (27%)
  matrix products  55.3 us (10%)
  local copies, waits for them, and re-layouts  44.1 us (8%)
  starting transfers between devices  25.6 us (5%)
  other arithmetic  16.8 us (3%)
  between operations  14.9 us (3%)
  loops' own time  12.9 us (2%)
    all_gather x1, waiting for transfers between devices, side_by_side(): out = lax.all_gather(both, axis, axis=dim, tiled=True)  175 us
    all_gather x9, blocking collectives, turn(): features = lax.all_gather(hidden, 'tp', axis=1, tiled=True)  60.4 us
    ppermute x9, waiting for transfers between devices, from_behind(): return lax.ppermute(block, axis, route)  50.9 us
    all_gather x9, blocking collectives, turn(): every_head = lax.all_gather(heads_out, 'tp', axis=1, tiled=True)  50.7 us
    ppermute x9, starting transfers between devices, from_behind(): return lax.ppermute(block, axis, route)  25.6 us
    all_to_all x1, blocking collectives, copy_for_each(): return lax.all_to_all(copies, axis, split_axis=0, concat_axis=0, tiled=True)  23.4 us
    dot_general x4, matrix products, attend(): jnp.dot(normed, query_proj, preferred_element_type=jnp.float32)  20.6 us
    dot_general x4, matrix products, turn(): jnp.dot(every_head, out_proj, preferred_element_type=jnp.float32)  19.8 us
  transfers between devices with their start and end apart: 11, of which 8 were waited for; matrix products, arithmetic and copies ran while one was open for 7% of the time, Pallas kernels for 0%

commit v1 on v0

--- a/solution.py
+++ b/solution.py
@@ -3,6 +3,7 @@
 import jax.numpy as jnp
 from jax import lax
 from jax.sharding import PartitionSpec as P
+from jax.lax import all_to_all, axis_size
 
 HD = 128
 M = 16
@@ -10,6 +11,15 @@
 SEGS = 2
 EPSILON = 1e-05
 NEGATIVE = -1e30
+update_rates = lambda incoming_x, shard_axis: jnp.concatenate(
+    all_to_all(
+        jnp.stack([incoming_x for _ in range(axis_size(shard_axis))]),
+        shard_axis,
+        split_axis=0,
+        concat_axis=0,
+    ),
+    axis=1,
+)
 
 
 def side_by_side(arrays, axis, dim, along):
@@ -129,7 +139,7 @@
         memory = jnp.where(segment == 0, mem_init, earlier)
         hidden = jnp.where(phase_index == 0, jnp.concatenate([memory, tokens], 0), incoming)
         length = seg_lengths[document, segment]
-        features = lax.all_gather(hidden, "tp", axis=1, tiled=True)
+        features = update_rates(hidden, "tp")
         heads_out = lax.cond(
             active,
             lambda: attend(features, length, query_proj, key_proj, value_proj, norm_row),

time: 545 us -> 584 us (1.072)
  blocking collectives: 148 us -> 88.4 us
  starting transfers between devices: 25.6 us -> 74.7 us
  waiting for transfers between devices: 226 us -> 264 us
  other arithmetic: 16.8 us -> 27 us
    all_gather x9 -> x0, blocking collectives: 60.4 us -> none  [turn(): features = lax.all_gather(hidden, 'tp', axis=1, tiled=True)]
    all_to_all x0 -> x9, starting transfers between devices: none -> 47.3 us  [all_to_all(jnp.stack([incoming_x for _ in range(axis_size(shard_axis))]),...]
    all_to_all x0 -> x9, waiting for transfers between devices: none -> 19.1 us  [all_to_all(jnp.stack([incoming_x for _ in range(axis_size(shard_axis))]),...]
    ppermute x9, waiting for transfers between devices: 50.9 us -> 69.3 us  [from_behind(): return lax.ppermute(block, axis, route)]
    another operation x0 -> x18, other arithmetic: none -> 7.41 us  [jnp.stack([incoming_x for _ in range(axis_size(shard_axis))])]
  transfers between devices with their start and end apart: 11 -> 20, of which waited for: 8 -> 19; matrix products, arithmetic and copies ran while one was open for 7% -> 7% of each run, Pallas kernels for 0% -> 0%
where the time goes in v1:
time: 584 us; the launch traced here: 582 us
  waiting for transfers between devices  264 us (45%)
  blocking collectives  88.4 us (15%)
  starting transfers between devices  74.7 us (13%)
  matrix products  54.6 us (9%)
  local copies, waits for them, and re-layouts  46.4 us (8%)
  other arithmetic  27 us (5%)
  between operations  14.9 us (3%)
  loops' own time  12.1 us (2%)
    all_gather x1, waiting for transfers between devices, side_by_side(): out = lax.all_gather(both, axis, axis=dim, tiled=True)  175 us
    ppermute x9, waiting for transfers between devices, from_behind(): return lax.ppermute(block, axis, route)  69.3 us
    all_gather x9, blocking collectives, turn(): every_head = lax.all_gather(heads_out, 'tp', axis=1, tiled=True)  50.2 us
    all_to_all x9, starting transfers between devices, all_to_all(jnp.stack([incoming_x for _ in range(axis_size(shard_axis))]),...  47.3 us
    ppermute x9, starting transfers between devices, from_behind(): return lax.ppermute(block, axis, route)  27.4 us
    all_to_all x1, blocking collectives, copy_for_each(): return lax.all_to_all(copies, axis, split_axis=0, concat_axis=0, tiled=True)  23.4 us
    dot_general x4, matrix products, attend(): jnp.dot(normed, query_proj, preferred_element_type=jnp.float32)  20.5 us
    dot_general x4, matrix products, turn(): jnp.dot(every_head, out_proj, preferred_element_type=jnp.float32)  19.8 us
  transfers between devices with their start and end apart: 20, of which 19 were waited for; matrix products, arithmetic and copies ran while one was open for 7% of the time, Pallas kernels for 0%

profile of v1, /device:TPU:6, one launch (start us, length us, event | category | flops | bytes accessed | tf_op | source)
XLA Modules:
  0.0 582.1 jit_solution(11231503142627695007)
XLA Ops:
  11.2 9.4 %gather_fusion = bf16[128,2048]{1,0:T(8,128)(2,1)S(1)} fusion(bf16[4096,2048]{1,0:T(8,128)(2,1)} %param.18, s32[1024]{0:T(1024)S(1)} %pad_clamp_fusion), kind=kCustom, calls=%fused_computation | custom fusion | bytes 1049088 | tf_op jit(solution)/shard_map/jit(_take)/gather | solution.py:117
  21.8 175.4 %all-gather.2.cloned.1.call-done = bf16[4096,3072]{1,0:T(8,128)(2,1)} async-done(((bf16[128,3072]{1,0:T(8,128)(2,1)}), bf16[4096,3072]{1,0:T(8,128)(2,1)}) %all-gather.2.cloned.1.call-update) | async-done | bytes 25165840 | tf_op jit(solution)/shard_map/all_gather | solution.py:28
  197.2 16.9 %fusion.20 = (bf16[4096,1024]{1,0:T(8,128)(2,1)}, bf16[4096,1024]{1,0:T(8,128)(2,1)}, bf16[4096,1024]{1,0:T(8,128)(2,1)}) fusion(bf16[4096,3072]{1,0:T(8,128)(2,1)} %all-gather.2.cloned.1.call-done), kind=kLoop, calls=%fused_computation.52 | loop fusion | bytes 50331648 | tf_op jit(solution)/shard_map/split | solution.py:29
  214.2 320.8 %while.18 = (s32[]{:T(128)}, bf16[48,2048]{1,0:T(8,128)(2,1)S(1)}, f32[2,2048]{1,0:T(2,128)S(1)}, pred[]{:T(512)}, s32[]{:T(128)}, /*index=5*/bf16[16,2048]{1,0:...) while((s32[]{:T(128)}, bf16[48,2048]{1,0:T(8,128)(2,1)S(1)}, ...), condition=%wide.region_9.10_spmd.clone, body=%wide.region_1.9_spmd.clone.sunk | while | flops 1623443072 | bytes 96115064 | solution.py:170
  224.7 5.3 all_gather.16
  230.4 6.4 %collective-permute-done = bf16[48,2048]{1,0:T(8,128)(2,1)S(1)} collective-permute-done((bf16[48,2048]{1,0:T(8,128)(2,1)S(1)}, bf16[48,2048]{1,0:T(8,128)(2,1)S(1)}, u32[]{:S(2)}, u32[]{:S(2)}) %collective-permute-start) | collective-permute-done | bytes 196640 | tf_op jit(solution)/shard_map/while/body/eval_jaxpr/ppermute | solution.py:35
  238.5 5.2 all-to-all-start
  247.6 5.7 all_gather.16
  253.4 11.5 %collective-permute-start = (bf16[48,2048]{1,0:T(8,128)(2,1)S(1)}, bf16[48,2048]{1,0:T(8,128)(2,1)S(1)}, u32[]{:S(2)}, u32[]{:S(2)}) collective-permute-start(bf16[48,2048]{1,0:T(8,128)(2,1)S(1)} %add_convert_fusion.2), channel_id=1, source_target_pairs={{192,0},{0,64},{64,128},{128,192},{193,1},{1,65},{65,129},{129,193... | collective-permute-start | bytes 589832 | tf_op jit(solution)/shard_map/while/body/eval_jaxpr/ppermute | solution.py:35
  265.1 19.4 %collective-permute-done = bf16[48,2048]{1,0:T(8,128)(2,1)S(1)} collective-permute-done((bf16[48,2048]{1,0:T(8,128)(2,1)S(1)}, bf16[48,2048]{1,0:T(8,128)(2,1)S(1)}, u32[]{:S(2)}, u32[]{:S(2)}) %collective-permute-start) | collective-permute-done | bytes 196640 | tf_op jit(solution)/shard_map/while/body/eval_jaxpr/ppermute | solution.py:35
  295.8 11.9 %conditional.6 = (bf16[48,1024]{1,0:T(8,128)(2,1)S(1)}) conditional(s32[]{:T(128)} %convert_element_type.144, () %tuple.66, (bf16[48,2,2048]{2,0,1:T(8,128)(2,1)S(1)}, f32[1,4096]{1,0:T(1,128)S(1)}, bf16[4096,1024]{1,0:T(8,128)(2,1)}, s32[]{:T(128)}, bf16[4096,1024]{1,0:T(8,128)(2,1)}, /*index=5*/bf16[4096,1024]{1,0:T(8,128)(2,1)}) %tuple.81), branch_computations={%region_2.2_spmd, %region_3.5_spmd} | conditional | flops 1219071616 | bytes 82056752 | solution.py:143
  297.5 5.1 fusion.5
  307.7 5.3 all_gather.16
  313.0 4.9 conditional.7
  313.0 4.9 fusion.21
  318.3 6.7 %collective-permute-done = bf16[48,2048]{1,0:T(8,128)(2,1)S(1)} collective-permute-done((bf16[48,2048]{1,0:T(8,128)(2,1)S(1)}, bf16[48,2048]{1,0:T(8,128)(2,1)S(1)}, u32[]{:S(2)}, u32[]{:S(2)}) %collective-permute-start) | collective-permute-done | bytes 196640 | tf_op jit(solution)/shard_map/while/body/eval_jaxpr/ppermute | solution.py:35
  326.7 4.6 all-to-all-start
  335.2 11.9 %conditional.6 = (bf16[48,1024]{1,0:T(8,128)(2,1)S(1)}) conditional(s32[]{:T(128)} %convert_element_type.144, () %tuple.66, (bf16[48,2,2048]{2,0,1:T(8,128)(2,1)S(1)}, f32[1,4096]{1,0:T(1,128)S(1)}, bf16[4096,1024]{1,0:T(8,128)(2,1)}, s32[]{:T(128)}, bf16[4096,1024]{1,0:T(8,128)(2,1)}, /*index=5*/bf16[4096,1024]{1,0:T(8,128)(2,1)}) %tuple.81), branch_computations={%region_2.2_spmd, %region_3.5_spmd} | conditional | flops 1219071616 | bytes 82056752 | solution.py:143
  336.9 5.1 fusion.5
  347.1 5.9 %all_gather.16 = bf16[48,2048]{1,0:T(8,128)(2,1)S(1)} all-gather(bf16[48,1024]{1,0:T(8,128)(2,1)S(1)} %get-tuple-element.606), channel_id=1, replica_groups=mesh['section'=4,'tp'=2,'doc'=32] {'tp'}, dimensions={1}, use_global_device_ids=true | all-gather | bytes 294912 | tf_op jit(solution)/shard_map/while/body/eval_jaxpr/all_gather | solution.py:148
  353.0 4.9 conditional.7
  353.0 4.9 fusion.21
  358.3 6.4 %collective-permute-done = bf16[48,2048]{1,0:T(8,128)(2,1)S(1)} collective-permute-done((bf16[48,2048]{1,0:T(8,128)(2,1)S(1)}, bf16[48,2048]{1,0:T(8,128)(2,1)S(1)}, u32[]{:S(2)}, u32[]{:S(2)}) %collective-permute-start) | collective-permute-done | bytes 196640 | tf_op jit(solution)/shard_map/while/body/eval_jaxpr/ppermute | solution.py:35
  366.4 7.5 %all-to-all-start = ((bf16[2,48,2048]{2,1,0:T(8,128)(2,1)}), bf16[2,48,2048]{2,1,0:T(8,128)(2,1)S(1)}, u32[]{:S(2)}, u32[]{:S(2)}) async-start(bf16[2,48,2048]{2,1,0:T(8,128)(2,1)} %pad_maximum_fusion.3), calls=%async_computation | async-start | bytes 786432 | tf_op jit(solution)/shard_map/while/body/eval_jaxpr/all_to_all | solution.py:15
  377.8 5.3 all_gather.16
  383.2 7.8 %collective-permute-start = (bf16[48,2048]{1,0:T(8,128)(2,1)S(1)}, bf16[48,2048]{1,0:T(8,128)(2,1)S(1)}, u32[]{:S(2)}, u32[]{:S(2)}) collective-permute-start(bf16[48,2048]{1,0:T(8,128)(2,1)S(1)} %add_convert_fusion.2), channel_id=1, source_target_pairs={{192,0},{0,64},{64,128},{128,192},{193,1},{1,65},{65,129},{129,193... | collective-permute-start | bytes 589832 | tf_op jit(solution)/shard_map/while/body/eval_jaxpr/ppermute | solution.py:35
  393.8 5.2 all-to-all-start
  404.2 6.3 %all_gather.16 = bf16[48,2048]{1,0:T(8,128)(2,1)S(1)} all-gather(bf16[48,1024]{1,0:T(8,128)(2,1)S(1)} %get-tuple-element.606), channel_id=1, replica_groups=mesh['section'=4,'tp'=2,'doc'=32] {'tp'}, dimensions={1}, use_global_device_ids=true | all-gather | bytes 294912 | tf_op jit(solution)/shard_map/while/body/eval_jaxpr/all_gather | solution.py:148
  410.9 15.7 %collective-permute-done = bf16[48,2048]{1,0:T(8,128)(2,1)S(1)} collective-permute-done((bf16[48,2048]{1,0:T(8,128)(2,1)S(1)}, bf16[48,2048]{1,0:T(8,128)(2,1)S(1)}, u32[]{:S(2)}, u32[]{:S(2)}) %collective-permute-start) | collective-permute-done | bytes 196640 | tf_op jit(solution)/shard_map/while/body/eval_jaxpr/ppermute | solution.py:35
  428.4 4.4 all-to-all-start
  438.6 11.9 %conditional.6 = (bf16[48,1024]{1,0:T(8,128)(2,1)S(1)}) conditional(s32[]{:T(128)} %convert_element_type.144, () %tuple.66, (bf16[48,2,2048]{2,0,1:T(8,128)(2,1)S(1)}, f32[1,4096]{1,0:T(1,128)S(1)}, bf16[4096,1024]{1,0:T(8,128)(2,1)}, s32[]{:T(128)}, bf16[4096,1024]{1,0:T(8,128)(2,1)}, /*index=5*/bf16[4096,1024]{1,0:T(8,128)(2,1)}) %tuple.81), branch_computations={%region_2.2_spmd, %region_3.5_spmd} | conditional | flops 1219071616 | bytes 82056752 | solution.py:143
  440.3 5.1 fusion.5
  450.4 5.3 all_gather.16
  455.7 4.9 conditional.7
  455.7 4.9 fusion.21
  461.0 6.7 %collective-permute-done = bf16[48,2048]{1,0:T(8,128)(2,1)S(1)} collective-permute-done((bf16[48,2048]{1,0:T(8,128)(2,1)S(1)}, bf16[48,2048]{1,0:T(8,128)(2,1)S(1)}, u32[]{:S(2)}, u32[]{:S(2)}) %collective-permute-start) | collective-permute-done | bytes 196640 | tf_op jit(solution)/shard_map/while/body/eval_jaxpr/ppermute | solution.py:35
  469.5 4.6 all-to-all-start
  477.9 11.9 %conditional.6 = (bf16[48,1024]{1,0:T(8,128)(2,1)S(1)}) conditional(s32[]{:T(128)} %convert_element_type.144, () %tuple.66, (bf16[48,2,2048]{2,0,1:T(8,128)(2,1)S(1)}, f32[1,4096]{1,0:T(1,128)S(1)}, bf16[4096,1024]{1,0:T(8,128)(2,1)}, s32[]{:T(128)}, bf16[4096,1024]{1,0:T(8,128)(2,1)}, /*index=5*/bf16[4096,1024]{1,0:T(8,128)(2,1)}) %tuple.81), branch_computations={%region_2.2_spmd, %region_3.5_spmd} | conditional | flops 1219071616 | bytes 82056752 | solution.py:143
  479.6 5.1 fusion.5
  489.8 5.8 all_gather.16
  495.6 4.9 conditional.7
  495.6 4.9 fusion.21
  500.9 6.4 %collective-permute-done = bf16[48,2048]{1,0:T(8,128)(2,1)S(1)} collective-permute-done((bf16[48,2048]{1,0:T(8,128)(2,1)S(1)}, bf16[48,2048]{1,0:T(8,128)(2,1)S(1)}, u32[]{:S(2)}, u32[]{:S(2)}) %collective-permute-start) | collective-permute-done | bytes 196640 | tf_op jit(solution)/shard_map/while/body/eval_jaxpr/ppermute | solution.py:35
  509.0 8.0 %all-to-all-start = ((bf16[2,48,2048]{2,1,0:T(8,128)(2,1)}), bf16[2,48,2048]{2,1,0:T(8,128)(2,1)S(1)}, u32[]{:S(2)}, u32[]{:S(2)}) async-start(bf16[2,48,2048]{2,1,0:T(8,128)(2,1)} %pad_maximum_fusion.3), calls=%async_computation | async-start | bytes 786432 | tf_op jit(solution)/shard_map/while/body/eval_jaxpr/all_to_all | solution.py:15
  520.9 5.3 all_gather.16
  526.3 7.6 %collective-permute-start = (bf16[48,2048]{1,0:T(8,128)(2,1)S(1)}, bf16[48,2048]{1,0:T(8,128)(2,1)S(1)}, u32[]{:S(2)}, u32[]{:S(2)}) collective-permute-start(bf16[48,2048]{1,0:T(8,128)(2,1)S(1)} %add_convert_fusion.2), channel_id=1, source_target_pairs={{192,0},{0,64},{64,128},{128,192},{193,1},{1,65},{65,129},{129,193... | collective-permute-start | bytes 589832 | tf_op jit(solution)/shard_map/while/body/eval_jaxpr/ppermute | solution.py:35
  535.0 14.8 %psum.15 = f32[2,2048]{1,0:T(2,128)S(1)} all-reduce(f32[2,2048]{1,0:T(2,128)S(1)} %get-tuple-element.367), channel_id=1, replica_groups=mesh['section'=4,'tp'=2,'doc'=32] {'section'}, use_global_device_ids=true, to_apply=%region_10.11 | all-reduce | flops 4096 | bytes 32768 | tf_op jit(solution)/shard_map/psum | solution.py:172
  550.0 23.4 %all_to_all.19 = f32[32,2,2048]{2,1,0:T(2,128)S(1)} all-to-all(f32[32,2,2048]{2,1,0:T(2,128)S(1)} %broadcast_in_dim.106), channel_id=1, replica_groups=mesh['section'=4,'tp'=2,'doc'=32] {'doc'}, dimensions={0} | all-to-all | bytes 1048576 | tf_op jit(solution)/shard_map/all_to_all | solution.py:46
  (251 shorter events, 90.9 us)
Async XLA Ops:
  7.4 189.8 %all-gather.2.cloned.1.call-start = ((), (), s32[]{:S(2)}) async-start(), calls=%async_computation.3 | async-start | bytes 25952256 | tf_op jit(solution)/shard_map/all_gather | solution.py:28
  9.5 204.6 %all-reduce.2.cloned.1.call-start = ((), (), s32[]{:S(2)}) async-start(), calls=%async_computation.2 | async-start | bytes 1048576 | tf_op jit(solution)/shard_map/psum | solution.py:119
  21.7 192.4 %copy-start = (bf16[16,2048]{1,0:T(8,128)(2,1)S(1)}, bf16[16,2048]{1,0:T(8,128)(2,1)}, u32[]{:S(2)}) copy-start(bf16[16,2048]{1,0:T(8,128)(2,1)} %param.19) | copy-start | bytes 196612
  21.8 192.4 %copy-start.1 = (f32[1,4096]{1,0:T(1,128)S(1)}, f32[1,4096]{1,0:T(1,128)}, u32[]{:S(2)}) copy-start(f32[1,4096]{1,0:T(1,128)} %param.20) | copy-start | bytes 49156
  21.8 192.4 %copy-start.2 = (s32[2,2]{1,0:T(2,128)S(1)}, s32[2,2]{1,0:T(2,128)}, u32[]{:S(2)}) copy-start(s32[2,2]{1,0:T(2,128)} %param.17) | copy-start | bytes 52
  216.0 8.7 %all-to-all-start = ((bf16[2,48,2048]{2,1,0:T(8,128)(2,1)}), bf16[2,48,2048]{2,1,0:T(8,128)(2,1)S(1)}, u32[]{:S(2)}, u32[]{:S(2)}) async-start(bf16[2,48,2048]{2,1,0:T(8,128)(2,1)} %pad_maximum_fusion.3), calls=%async_computation | async-start | bytes 786432 | tf_op jit(solution)/shard_map/while/body/eval_jaxpr/all_to_all | solution.py:15
  230.1 6.7 %collective-permute-start = (bf16[48,2048]{1,0:T(8,128)(2,1)S(1)}, bf16[48,2048]{1,0:T(8,128)(2,1)S(1)}, u32[]{:S(2)}, u32[]{:S(2)}) collective-permute-start(bf16[48,2048]{1,0:T(8,128)(2,1)S(1)} %add_convert_fusion.2), channel_id=1, source_target_pairs={{192,0},{0,64},{64,128},{128,192},{193,1},{1,65},{65,129},{129,193... | collective-permute-start | bytes 589832 | tf_op jit(solution)/shard_map/while/body/eval_jaxpr/ppermute | solution.py:35
  238.5 9.1 %all-to-all-start = ((bf16[2,48,2048]{2,1,0:T(8,128)(2,1)}), bf16[2,48,2048]{2,1,0:T(8,128)(2,1)S(1)}, u32[]{:S(2)}, u32[]{:S(2)}) async-start(bf16[2,48,2048]{2,1,0:T(8,128)(2,1)} %pad_maximum_fusion.3), calls=%async_computation | async-start | bytes 786432 | tf_op jit(solution)/shard_map/while/body/eval_jaxpr/all_to_all | solution.py:15
  253.4 31.1 %collective-permute-start = (bf16[48,2048]{1,0:T(8,128)(2,1)S(1)}, bf16[48,2048]{1,0:T(8,128)(2,1)S(1)}, u32[]{:S(2)}, u32[]{:S(2)}) collective-permute-start(bf16[48,2048]{1,0:T(8,128)(2,1)S(1)} %add_convert_fusion.2), channel_id=1, source_target_pairs={{192,0},{0,64},{64,128},{128,192},{193,1},{1,65},{65,129},{129,193... | collective-permute-start | bytes 589832 | tf_op jit(solution)/shard_map/while/body/eval_jaxpr/ppermute | solution.py:35
  286.4 9.5 %all-to-all-start = ((bf16[2,48,2048]{2,1,0:T(8,128)(2,1)}), bf16[2,48,2048]{2,1,0:T(8,128)(2,1)S(1)}, u32[]{:S(2)}, u32[]{:S(2)}) async-start(bf16[2,48,2048]{2,1,0:T(8,128)(2,1)} %pad_maximum_fusion.3), calls=%async_computation | async-start | bytes 786432 | tf_op jit(solution)/shard_map/while/body/eval_jaxpr/all_to_all | solution.py:15
  297.4 5.3 slice-start
  297.5 5.7 slice-start.1
  297.5 8.2 %slice-start.2 = ((s8[8388608]{0:T(1024)(128)(4,1)}), s8[4194304]{0:T(1024)(128)(4,1)S(1)}, s32[]{:S(2)}) async-start(s8[8388608]{0:T(1024)(128)(4,1)} %bitcast.57), calls=%async_computation.6 | async-start | bytes 8388608 | tf_op jit(solution)/shard_map/while/body/eval_jaxpr/cond
  303.3 2.6 slice-start.3
  318.0 7.0 %collective-permute-start = (bf16[48,2048]{1,0:T(8,128)(2,1)S(1)}, bf16[48,2048]{1,0:T(8,128)(2,1)S(1)}, u32[]{:S(2)}, u32[]{:S(2)}) collective-permute-start(bf16[48,2048]{1,0:T(8,128)(2,1)S(1)} %add_convert_fusion.2), channel_id=1, source_target_pairs={{192,0},{0,64},{64,128},{128,192},{193,1},{1,65},{65,129},{129,193... | collective-permute-start | bytes 589832 | tf_op jit(solution)/shard_map/while/body/eval_jaxpr/ppermute | solution.py:35
  326.7 8.5 %all-to-all-start = ((bf16[2,48,2048]{2,1,0:T(8,128)(2,1)}), bf16[2,48,2048]{2,1,0:T(8,128)(2,1)S(1)}, u32[]{:S(2)}, u32[]{:S(2)}) async-start(bf16[2,48,2048]{2,1,0:T(8,128)(2,1)} %pad_maximum_fusion.3), calls=%async_computation | async-start | bytes 786432 | tf_op jit(solution)/shard_map/while/body/eval_jaxpr/all_to_all | solution.py:15
  336.7 5.3 slice-start
  336.9 5.7 slice-start.1
  336.9 8.2 %slice-start.2 = ((s8[8388608]{0:T(1024)(128)(4,1)}), s8[4194304]{0:T(1024)(128)(4,1)S(1)}, s32[]{:S(2)}) async-start(s8[8388608]{0:T(1024)(128)(4,1)} %bitcast.57), calls=%async_computation.6 | async-start | bytes 8388608 | tf_op jit(solution)/shard_map/while/body/eval_jaxpr/cond
  342.6 2.6 slice-start.3
  358.0 6.7 %collective-permute-start = (bf16[48,2048]{1,0:T(8,128)(2,1)S(1)}, bf16[48,2048]{1,0:T(8,128)(2,1)S(1)}, u32[]{:S(2)}, u32[]{:S(2)}) collective-permute-start(bf16[48,2048]{1,0:T(8,128)(2,1)S(1)} %add_convert_fusion.2), channel_id=1, source_target_pairs={{192,0},{0,64},{64,128},{128,192},{193,1},{1,65},{65,129},{129,193... | collective-permute-start | bytes 589832 | tf_op jit(solution)/shard_map/while/body/eval_jaxpr/ppermute | solution.py:35
  366.4 11.4 %all-to-all-start = ((bf16[2,48,2048]{2,1,0:T(8,128)(2,1)}), bf16[2,48,2048]{2,1,0:T(8,128)(2,1)S(1)}, u32[]{:S(2)}, u32[]{:S(2)}) async-start(bf16[2,48,2048]{2,1,0:T(8,128)(2,1)} %pad_maximum_fusion.3), calls=%async_computation | async-start | bytes 786432 | tf_op jit(solution)/shard_map/while/body/eval_jaxpr/all_to_all | solution.py:15
  383.2 8.8 %collective-permute-start = (bf16[48,2048]{1,0:T(8,128)(2,1)S(1)}, bf16[48,2048]{1,0:T(8,128)(2,1)S(1)}, u32[]{:S(2)}, u32[]{:S(2)}) collective-permute-start(bf16[48,2048]{1,0:T(8,128)(2,1)S(1)} %add_convert_fusion.2), channel_id=1, source_target_pairs={{192,0},{0,64},{64,128},{128,192},{193,1},{1,65},{65,129},{129,193... | collective-permute-start | bytes 589832 | tf_op jit(solution)/shard_map/while/body/eval_jaxpr/ppermute | solution.py:35
  393.8 10.3 %all-to-all-start = ((bf16[2,48,2048]{2,1,0:T(8,128)(2,1)}), bf16[2,48,2048]{2,1,0:T(8,128)(2,1)S(1)}, u32[]{:S(2)}, u32[]{:S(2)}) async-start(bf16[2,48,2048]{2,1,0:T(8,128)(2,1)} %pad_maximum_fusion.3), calls=%async_computation | async-start | bytes 786432 | tf_op jit(solution)/shard_map/while/body/eval_jaxpr/all_to_all | solution.py:15
  410.6 16.0 %collective-permute-start = (bf16[48,2048]{1,0:T(8,128)(2,1)S(1)}, bf16[48,2048]{1,0:T(8,128)(2,1)S(1)}, u32[]{:S(2)}, u32[]{:S(2)}) collective-permute-start(bf16[48,2048]{1,0:T(8,128)(2,1)S(1)} %add_convert_fusion.2), channel_id=1, source_target_pairs={{192,0},{0,64},{64,128},{128,192},{193,1},{1,65},{65,129},{129,193... | collective-permute-start | bytes 589832 | tf_op jit(solution)/shard_map/while/body/eval_jaxpr/ppermute | solution.py:35
  428.4 10.2 %all-to-all-start = ((bf16[2,48,2048]{2,1,0:T(8,128)(2,1)}), bf16[2,48,2048]{2,1,0:T(8,128)(2,1)S(1)}, u32[]{:S(2)}, u32[]{:S(2)}) async-start(bf16[2,48,2048]{2,1,0:T(8,128)(2,1)} %pad_maximum_fusion.3), calls=%async_computation | async-start | bytes 786432 | tf_op jit(solution)/shard_map/while/body/eval_jaxpr/all_to_all | solution.py:15
  440.1 5.3 slice-start
  440.2 5.7 slice-start.1
  440.2 8.2 %slice-start.2 = ((s8[8388608]{0:T(1024)(128)(4,1)}), s8[4194304]{0:T(1024)(128)(4,1)S(1)}, s32[]{:S(2)}) async-start(s8[8388608]{0:T(1024)(128)(4,1)} %bitcast.57), calls=%async_computation.6 | async-start | bytes 8388608 | tf_op jit(solution)/shard_map/while/body/eval_jaxpr/cond
  446.0 2.6 slice-start.3
  460.7 7.0 %collective-permute-start = (bf16[48,2048]{1,0:T(8,128)(2,1)S(1)}, bf16[48,2048]{1,0:T(8,128)(2,1)S(1)}, u32[]{:S(2)}, u32[]{:S(2)}) collective-permute-start(bf16[48,2048]{1,0:T(8,128)(2,1)S(1)} %add_convert_fusion.2), channel_id=1, source_target_pairs={{192,0},{0,64},{64,128},{128,192},{193,1},{1,65},{65,129},{129,193... | collective-permute-start | bytes 589832 | tf_op jit(solution)/shard_map/while/body/eval_jaxpr/ppermute | solution.py:35
  469.5 8.4 %all-to-all-start = ((bf16[2,48,2048]{2,1,0:T(8,128)(2,1)}), bf16[2,48,2048]{2,1,0:T(8,128)(2,1)S(1)}, u32[]{:S(2)}, u32[]{:S(2)}) async-start(bf16[2,48,2048]{2,1,0:T(8,128)(2,1)} %pad_maximum_fusion.3), calls=%async_computation | async-start | bytes 786432 | tf_op jit(solution)/shard_map/while/body/eval_jaxpr/all_to_all | solution.py:15
  479.5 5.3 slice-start
  479.6 5.7 slice-start.1
  479.6 8.2 %slice-start.2 = ((s8[8388608]{0:T(1024)(128)(4,1)}), s8[4194304]{0:T(1024)(128)(4,1)S(1)}, s32[]{:S(2)}) async-start(s8[8388608]{0:T(1024)(128)(4,1)} %bitcast.57), calls=%async_computation.6 | async-start | bytes 8388608 | tf_op jit(solution)/shard_map/while/body/eval_jaxpr/cond
  485.3 2.6 slice-start.3
  500.6 6.7 %collective-permute-start = (bf16[48,2048]{1,0:T(8,128)(2,1)S(1)}, bf16[48,2048]{1,0:T(8,128)(2,1)S(1)}, u32[]{:S(2)}, u32[]{:S(2)}) collective-permute-start(bf16[48,2048]{1,0:T(8,128)(2,1)S(1)} %add_convert_fusion.2), channel_id=1, source_target_pairs={{192,0},{0,64},{64,128},{128,192},{193,1},{1,65},{65,129},{129,193... | collective-permute-start | bytes 589832 | tf_op jit(solution)/shard_map/while/body/eval_jaxpr/ppermute | solution.py:35
  509.0 11.9 %all-to-all-start = ((bf16[2,48,2048]{2,1,0:T(8,128)(2,1)}), bf16[2,48,2048]{2,1,0:T(8,128)(2,1)S(1)}, u32[]{:S(2)}, u32[]{:S(2)}) async-start(bf16[2,48,2048]{2,1,0:T(8,128)(2,1)} %pad_maximum_fusion.3), calls=%async_computation | async-start | bytes 786432 | tf_op jit(solution)/shard_map/while/body/eval_jaxpr/all_to_all | solution.py:15
  526.3 8.7 %collective-permute-start = (bf16[48,2048]{1,0:T(8,128)(2,1)S(1)}, bf16[48,2048]{1,0:T(8,128)(2,1)S(1)}, u32[]{:S(2)}, u32[]{:S(2)}) collective-permute-start(bf16[48,2048]{1,0:T(8,128)(2,1)S(1)} %add_convert_fusion.2), channel_id=1, source_target_pairs={{192,0},{0,64},{64,128},{128,192},{193,1},{1,65},{65,129},{129,193... | collective-permute-start | bytes 589832 | tf_op jit(solution)/shard_map/while/body/eval_jaxpr/ppermute | solution.py:35
Sparse Core Ops, SparseCore 0:
  10.7 186.3 all-gather.1
Sparse Core Ops, SparseCore 1:
  21.8 48.7 all-reduce.1
